TPU v7x, 256 devices: a whole 4x4x8 slice. The times are simulated.
256 devices in a mesh: gy: 32 (over z, y), gx: 8 (over x, core).
Axes of the slice: x: 4, y: 4, z: 8, core: 2. Of those that a mesh axis runs over, the one named last changes fastest.
Arguments:
- bins: int32 [4, 512, 8192], P(None, 'gy', 'gx'), may hold values from 0 to 4095
- mask: int32 [4, 512, 8192], P(None, 'gy', 'gx'), may hold values from 0 to 1
- atlas: bfloat16 [8, 4, 512, 8192], P(None, None, 'gy', 'gx'), may hold values from -100 to 130
- init_mean: float32 [8], replicated, may hold values from 0.05 to 0.95
- init_scale: float32 [8], replicated, may hold values from 0.004 to 0.15
Outputs:
- phase_prob: bfloat16 [8, 4, 512, 8192], P(None, None, 'gy', 'gx')
- em_params: float32 [3, 8], replicated
- bin_density: float32 [4096], P(('gy', 'gx'))
All inputs are finite; a program needn't handle non-finite values.
Results may differ from a plain program's by a relative error of at most 0.0015.
Values may be sent and summed in bfloat16 or wider, within the bound.
A program may use at most 64 MiB of HBM per device.

v0:
```python
import math
import jax
import jax.numpy as jnp
from jax import lax
from jax.sharding import PartitionSpec as P

NB = 4096
EM_ITERS = 5
POTTS = 3
VAR_EPS = 1e-05
BETA = 0.3


def extended(x, sides, width):
    for axis, dim in sides:
        size, length = (lax.axis_size(axis), x.shape[dim])
        up = [(i, (i + 1) % size) for i in range(size - 1)]
        down = [(j, i) for i, j in up]
        last = lax.slice_in_dim(x, length - width, length, axis=dim)
        initial = lax.slice_in_dim(x, 0, width, axis=dim)
        before = lax.ppermute(last, axis, up)
        after = lax.ppermute(initial, axis, down)
        x = jnp.concatenate([before, x, after], axis=dim)
    return x


def phase_scores(values, mean, var, weight):
    shape = (mean.shape[0],) + (1,) * values.ndim
    m = mean.reshape(shape)
    v = var.reshape(shape)
    w = weight.reshape(shape)
    diff = values[None] - m
    return jnp.log(w) - 0.5 * jnp.log(v) - diff * diff / (2.0 * v)


def moments(counts, centers, mean, var, weight):
    resp = jax.nn.softmax(phase_scores(centers, mean, var, weight), axis=0)
    weighted = resp * counts[None]
    return jnp.stack(
        [
            jnp.sum(weighted, 1),
            jnp.sum(weighted * centers[None], 1),
            jnp.sum(weighted * (centers * centers)[None], 1),
        ]
    )


def refit(sums, count_phases):
    occ, first, second = (sums[0], sums[1], sums[2])
    mean = first / (occ + 1.0)
    var = (second - first * mean) / (occ + 1.0) + VAR_EPS
    weight = (occ + 1.0) / (jnp.sum(occ) + count_phases)
    return (mean, var, weight)


def cycle_total(padded, rows, cols):
    total = jnp.zeros(padded.shape[:2] + (rows, cols), jnp.float32)
    for dy in range(-2, 3):
        for dx in range(-2, 3):
            if dy != 0 or dx != 0:
                piece = padded[:, :, 2 + dy : 2 + dy + rows, 2 + dx : 2 + dx + cols].astype(
                    jnp.float32
                )
                total = total + piece * (1.0 / (dy * dy + dx * dx))
    return total


def plane_total(held):
    padded = jnp.pad(held.astype(jnp.float32), ((0, 0), (1, 1), (0, 0), (0, 0)))
    return padded[:, :-2] + padded[:, 2:]


def per_device(bins, mask, atlas, init_mean, init_scale):
    planes, rows, cols = bins.shape
    phases = init_mean.shape[0]
    devices_all = lax.axis_size("gy") * lax.axis_size("gx")
    scale_factor = float(NB) / float(planes * rows * cols * devices_all)
    group = math.gcd(16, planes * rows)
    block_bins = bins.reshape(-1, group * cols)
    block_mask = mask.reshape(-1, group * cols)
    high_count = NB // 128

    def count_block(acc, item):
        part_bins, part_mask = item
        high = part_bins // 128
        low = part_bins % 128
        high_hot = (high[None, :] == jnp.arange(high_count, dtype=jnp.int32)[:, None]).astype(
            jnp.bfloat16
        )
        high_hot = high_hot * part_mask.astype(jnp.bfloat16)[None, :]
        low_hot = (low[None, :] == jnp.arange(128, dtype=jnp.int32)[:, None]).astype(jnp.bfloat16)
        table = lax.dot_general(
            high_hot, low_hot, (((1,), (1,)), ((), ())), preferred_element_type=jnp.float32
        )
        return (acc + table, None)

    table, _ = lax.scan(
        count_block, jnp.zeros((high_count, 128), jnp.float32), (block_bins, block_mask)
    )
    counts = table.reshape(NB)
    mean = init_mean
    var = init_scale * init_scale
    weight = jnp.full((phases,), 1.0 / phases, jnp.float32)
    share = lax.psum_scatter(counts, ("gy", "gx"), scatter_dimension=0, tiled=True)
    start = lax.axis_index(("gy", "gx")) * share.shape[0]
    density = share * scale_factor
    centers = ((start + jnp.arange(share.shape[0], dtype=jnp.int32)).astype(jnp.float32) + 0.5) / NB
    for step in range(EM_ITERS):
        sums = lax.psum(moments(share, centers, mean, var, weight), ("gy", "gx"))
        mean, var, weight = refit(sums, float(phases))
    params = jnp.stack([mean, var, weight])
    intensity = (bins.astype(jnp.float32) + 0.5) / NB
    unary = phase_scores(intensity, mean, var, weight) + atlas.astype(jnp.float32)
    fg = mask.astype(jnp.float32)
    q = jax.nn.softmax(unary, axis=0).astype(jnp.bfloat16)
    for step in range(POTTS):
        held = (q.astype(jnp.float32) * fg[None]).astype(jnp.bfloat16)
        padded = extended(held, (("gy", 2), ("gx", 3)), 2)
        field = cycle_total(padded, rows, cols) + plane_total(held)
        q = jax.nn.softmax(unary + BETA * field, axis=0).astype(jnp.bfloat16)
    phase_prob = (q.astype(jnp.float32) * fg[None]).astype(jnp.bfloat16)
    return (phase_prob, params, density)


def solution(mesh):
    in_specs = (P(None, "gy", "gx"), P(None, "gy", "gx"), P(None, None, "gy", "gx"), P(), P())
    out_specs = (P(None, None, "gy", "gx"), P(), P(("gy", "gx")))
    return jax.shard_map(
        per_device, mesh=mesh, in_specs=in_specs, out_specs=out_specs, check_vma=False
    )
```

profile of v0, /device:TPU:121, one launch (start us, length us, event | category | flops | bytes accessed | tf_op | source)
XLA Modules:
  0.0 586.1 jit_solution(10782457312624884916)
XLA Ops:
  5.1 10.4 %while.13 = (s32[]{:T(128)}, f32[32,128]{1,0:T(8,128)S(1)}, s32[4,16384]{1,0:T(4,128)S(1)}, s32[4,16384]{1,0:T(4,128)S(1)}, s32[]{:T(128)}, /*index=5*/s32[]{:T(128)}) while((s32[]{:T(128)}, f32[32,128]{1,0:T(8,128)S(1)}, s32[4,16384]{1,0:T(4,128)S(1)}, s32[4,16384]{1,0:T(4,128)S(1)}, s32[]{:T(128)}, /*index=5*/s32[]{:T(128)}) %tuple.78), condition=%wide.region_3.4_spmd.clone, body=%wide.region_2.3_spmd.clone.sunk | while | flops 137715712 | bytes 2719839 | solution.py:97
  15.5 75.7 %all-reduce.3 = f32[4096]{0:T(1024)S(1)} all-reduce(f32[4096]{0:T(1024)S(1)} %bitcast.175), channel_id=2, replica_groups=mesh['gy'=32,'gx'=8] {'gy','gx'}, use_global_device_ids=true, to_apply=%region_4.5.clone | all-reduce | flops 4096 | bytes 32768
  92.1 73.5 %psum.35 = f32[3,8]{1,0:T(4,128)S(1)} all-reduce(f32[3,8]{1,0:T(4,128)S(1)} %pad_maximum_fusion.18), channel_id=1, replica_groups=mesh['gy'=32,'gx'=8] {'gy','gx'}, use_global_device_ids=true, to_apply=%region_8.9 | all-reduce | flops 24 | bytes 192 | tf_op jit(solution)/shard_map/psum | solution.py:109
  167.3 74.1 %psum.36 = f32[3,8]{1,0:T(4,128)S(1)} all-reduce(f32[3,8]{1,0:T(4,128)S(1)} %pad_maximum_fusion.19), channel_id=1, replica_groups=mesh['gy'=32,'gx'=8] {'gy','gx'}, use_global_device_ids=true, to_apply=%region_15.16 | all-reduce | flops 24 | bytes 192 | tf_op jit(solution)/shard_map/psum | solution.py:109
  243.1 73.5 %psum.37 = f32[3,8]{1,0:T(4,128)S(1)} all-reduce(f32[3,8]{1,0:T(4,128)S(1)} %pad_maximum_fusion.20), channel_id=1, replica_groups=mesh['gy'=32,'gx'=8] {'gy','gx'}, use_global_device_ids=true, to_apply=%region_22.23 | all-reduce | flops 24 | bytes 192 | tf_op jit(solution)/shard_map/psum | solution.py:109
  318.3 74.1 %psum.38 = f32[3,8]{1,0:T(4,128)S(1)} all-reduce(f32[3,8]{1,0:T(4,128)S(1)} %pad_maximum_fusion.21), channel_id=1, replica_groups=mesh['gy'=32,'gx'=8] {'gy','gx'}, use_global_device_ids=true, to_apply=%region_29.30 | all-reduce | flops 24 | bytes 192 | tf_op jit(solution)/shard_map/psum | solution.py:109
  394.2 73.5 %psum.39 = f32[3,8]{1,0:T(4,128)S(1)} all-reduce(f32[3,8]{1,0:T(4,128)S(1)} %pad_maximum_fusion.22), channel_id=1, replica_groups=mesh['gy'=32,'gx'=8] {'gy','gx'}, use_global_device_ids=true, to_apply=%region_36.37 | all-reduce | flops 24 | bytes 192 | tf_op jit(solution)/shard_map/psum | solution.py:109
  471.4 4.0 collective-permute-start
  477.6 6.8 %collective-permute-done.1 = bf16[8,4,2,1024]{3,2,1,0:T(2,128)(2,1)S(1)} collective-permute-done((bf16[8,4,2,1024]{3,2,1,0:T(2,128)(2,1)S(1)}, bf16[8,4,2,1024]{3,2,1,0:T(2,128)(2,1)S(1)}, u32[]{:S(2)}, u32[]{:S(2)}) %collective-permute-start.1) | collective-permute-done | bytes 131104 | tf_op jit(solution)/shard_map/ppermute | solution.py:22
  484.7 4.7 collective-permute-start.2
  492.0 4.4 collective-permute-done.3
  496.4 2.9 maximum_maximum_fusion
  499.2 11.3 %fusion.75 = (f32[4,16,1024]{2,1,0:T(8,128)S(1)}, f32[8,4,16,1024]{3,2,1,0:T(8,128)S(1)}) fusion(f32[8,6,16,1024]{3,2,1,0:T(8,128)S(1)} %pad_convert_fusion.2, bf16[8,4,20,1026]{3,2,1,0:T(8,128)(2,1)S(1)} %get-tuple-element.134, bf16[8,4,2,1024]{3,2,1,0:T(2,128)(2,1)S(1)} %collective-permute-done.1, bf16[8,4,16,1024]{3,2,1,0:T(8,128)(2,1)S(1)} %multiply_convert_fusion.3, ...), kind=kLoop, calls=%fused_computation.201 | loop fusion | flops 47120384 | bytes 30146656 | tf_op jit(solution)/shard_map/reduce_max | solution.py:120
  513.4 3.4 collective-permute-start.5
  517.2 5.2 collective-permute-done.5
  522.7 4.0 collective-permute-start.6
  529.3 4.4 collective-permute-done.7
  533.7 2.9 maximum_maximum_fusion.1
  536.5 11.3 %fusion.73 = (f32[4,16,1024]{2,1,0:T(8,128)S(1)}, f32[8,4,16,1024]{3,2,1,0:T(8,128)S(1)}) fusion(f32[8,6,16,1024]{3,2,1,0:T(8,128)S(1)} %pad_convert_fusion.1, bf16[8,4,20,1026]{3,2,1,0:T(8,128)(2,1)S(1)} %get-tuple-element.130, bf16[8,4,2,1024]{3,2,1,0:T(2,128)(2,1)S(1)} %collective-permute-done.5, bf16[8,4,16,1024]{3,2,1,0:T(8,128)(2,1)S(1)} %multiply_convert_fusion.2, ...), kind=kLoop, calls=%fused_computation.200 | loop fusion | flops 47120384 | bytes 30146656 | tf_op jit(solution)/shard_map/reduce_max | solution.py:120
  550.7 3.4 collective-permute-start.9
  554.7 5.1 collective-permute-done.9
  560.0 3.3 collective-permute-start.10
  565.9 4.4 collective-permute-done.11
  573.2 11.3 %fusion.71 = (f32[4,16,1024]{2,1,0:T(8,128)S(1)}, f32[8,4,16,1024]{3,2,1,0:T(8,128)S(1)}) fusion(f32[8,6,16,1024]{3,2,1,0:T(8,128)S(1)} %pad_convert_fusion, bf16[8,4,20,1026]{3,2,1,0:T(8,128)(2,1)S(1)} %get-tuple-element.126, bf16[8,4,2,1024]{3,2,1,0:T(2,128)(2,1)S(1)} %collective-permute-done.9, bf16[8,4,16,1024]{3,2,1,0:T(8,128)(2,1)S(1)} %multiply_convert_fusion.1, ...), kind=kLoop, calls=%fused_computation.199 | loop fusion | flops 47120384 | bytes 30146656 | tf_op jit(solution)/shard_map/reduce_max | solution.py:120
  (104 shorter events, 44.7 us)
Async XLA Ops:
  5.1 86.7 %copy-start.3 = (f32[8]{0:T(128)S(1)}, f32[8]{0:T(128)}, u32[]{:S(2)}) copy-start(f32[8]{0:T(128)} %param.10) | copy-start | bytes 100
  5.1 313.2 %copy-start.1 = (s32[4,16,1024]{2,1,0:T(8,128)S(1)}, s32[4,16,1024]{2,1,0:T(8,128)}, u32[]{:S(2)}) copy-start(s32[4,16,1024]{2,1,0:T(8,128)} %param.7) | copy-start | bytes 786436
  5.1 389.0 %copy-start.2 = (s32[4,16,1024]{2,1,0:T(8,128)S(1)}, s32[4,16,1024]{2,1,0:T(8,128)}, u32[]{:S(2)}) copy-start(s32[4,16,1024]{2,1,0:T(8,128)} %param.8) | copy-start | bytes 786436
  5.1 463.8 %copy-start = (bf16[8,4,16,1024]{3,2,1,0:T(8,128)(2,1)S(1)}, bf16[8,4,16,1024]{3,2,1,0:T(8,128)(2,1)}, u32[]{:S(2)}) copy-start(bf16[8,4,16,1024]{3,2,1,0:T(8,128)(2,1)} %param.9) | copy-start | bytes 3145732
  471.4 6.3 %collective-permute-start = (bf16[8,4,2,1024]{3,2,1,0:T(2,128)(2,1)S(1)}, bf16[8,4,2,1024]{3,2,1,0:T(2,128)(2,1)S(1)}, u32[]{:S(2)}, u32[]{:S(2)}) collective-permute-start(bf16[8,4,2,1024]{3,2,1,0:T(2,128)(2,1)S(1)} %get-tuple-element.141), channel_id=1, source_target_pairs={{0,8},{8,16},{16,24},{24,32},{32,40},{40,48},{48,56},{56,64},{64,7... | collective-permute-start | bytes 393224 | tf_op jit(solution)/shard_map/ppermute | solution.py:21
  475.4 9.0 %collective-permute-start.1 = (bf16[8,4,2,1024]{3,2,1,0:T(2,128)(2,1)S(1)}, bf16[8,4,2,1024]{3,2,1,0:T(2,128)(2,1)S(1)}, u32[]{:S(2)}, u32[]{:S(2)}) collective-permute-start(bf16[8,4,2,1024]{3,2,1,0:T(2,128)(2,1)S(1)} %get-tuple-element.142), channel_id=1, source_target_pairs={{8,0},{16,8},{24,16},{32,24},{40,32},{48,40},{56,48},{64,56},{72,6... | collective-permute-start | bytes 393224 | tf_op jit(solution)/shard_map/ppermute | solution.py:22
  484.7 7.3 %collective-permute-start.2 = (bf16[8,4,20,2]{3,2,1,0:T(8,128)(2,1)S(1)}, bf16[8,4,20,2]{3,2,1,0:T(8,128)(2,1)S(1)}, u32[]{:S(2)}, u32[]{:S(2)}) collective-permute-start(bf16[8,4,20,2]{3,2,1,0:T(8,128)(2,1)S(1)} %get-tuple-element.135), channel_id=1, source_target_pairs={{0,1},{1,2},{2,3},{3,4},{4,5},{5,6},{6,7},{8,9},{9,10},{10,11},{11... | collective-permute-start | bytes 7688 | tf_op jit(solution)/shard_map/ppermute | solution.py:21
  489.4 7.0 %collective-permute-start.3 = (bf16[8,4,20,2]{3,2,1,0:T(8,128)(2,1)S(1)}, bf16[8,4,20,2]{3,2,1,0:T(8,128)(2,1)S(1)}, u32[]{:S(2)}, u32[]{:S(2)}) collective-permute-start(bf16[8,4,20,2]{3,2,1,0:T(8,128)(2,1)S(1)} %get-tuple-element.136), channel_id=1, source_target_pairs={{1,0},{2,1},{3,2},{4,3},{5,4},{6,5},{7,6},{9,8},{10,9},{11,10},{12... | collective-permute-start | bytes 7688 | tf_op jit(solution)/shard_map/ppermute | solution.py:22
  511.5 5.7 collective-permute-start.4
  513.4 9.0 %collective-permute-start.5 = (bf16[8,4,2,1024]{3,2,1,0:T(2,128)(2,1)S(1)}, bf16[8,4,2,1024]{3,2,1,0:T(2,128)(2,1)S(1)}, u32[]{:S(2)}, u32[]{:S(2)}) collective-permute-start(bf16[8,4,2,1024]{3,2,1,0:T(2,128)(2,1)S(1)} %get-tuple-element.140), channel_id=1, source_target_pairs={{8,0},{16,8},{24,16},{32,24},{40,32},{48,40},{56,48},{64,56},{72,6... | collective-permute-start | bytes 393224 | tf_op jit(solution)/shard_map/ppermute | solution.py:22
  522.7 6.6 %collective-permute-start.6 = (bf16[8,4,20,2]{3,2,1,0:T(8,128)(2,1)S(1)}, bf16[8,4,20,2]{3,2,1,0:T(8,128)(2,1)S(1)}, u32[]{:S(2)}, u32[]{:S(2)}) collective-permute-start(bf16[8,4,20,2]{3,2,1,0:T(8,128)(2,1)S(1)} %get-tuple-element.131), channel_id=1, source_target_pairs={{0,1},{1,2},{2,3},{3,4},{4,5},{5,6},{6,7},{8,9},{9,10},{10,11},{11... | collective-permute-start | bytes 7688 | tf_op jit(solution)/shard_map/ppermute | solution.py:21
  526.7 7.0 %collective-permute-start.7 = (bf16[8,4,20,2]{3,2,1,0:T(8,128)(2,1)S(1)}, bf16[8,4,20,2]{3,2,1,0:T(8,128)(2,1)S(1)}, u32[]{:S(2)}, u32[]{:S(2)}) collective-permute-start(bf16[8,4,20,2]{3,2,1,0:T(8,128)(2,1)S(1)} %get-tuple-element.132), channel_id=1, source_target_pairs={{1,0},{2,1},{3,2},{4,3},{5,4},{6,5},{7,6},{9,8},{10,9},{11,10},{12... | collective-permute-start | bytes 7688 | tf_op jit(solution)/shard_map/ppermute | solution.py:22
  548.8 5.9 %collective-permute-start.8 = (bf16[8,4,2,1024]{3,2,1,0:T(2,128)(2,1)S(1)}, bf16[8,4,2,1024]{3,2,1,0:T(2,128)(2,1)S(1)}, u32[]{:S(2)}, u32[]{:S(2)}) collective-permute-start(bf16[8,4,2,1024]{3,2,1,0:T(2,128)(2,1)S(1)} %get-tuple-element.137), channel_id=1, source_target_pairs={{0,8},{8,16},{16,24},{24,32},{32,40},{40,48},{48,56},{56,64},{64,7... | collective-permute-start | bytes 393224 | tf_op jit(solution)/shard_map/ppermute | solution.py:21
  550.7 9.0 %collective-permute-start.9 = (bf16[8,4,2,1024]{3,2,1,0:T(2,128)(2,1)S(1)}, bf16[8,4,2,1024]{3,2,1,0:T(2,128)(2,1)S(1)}, u32[]{:S(2)}, u32[]{:S(2)}) collective-permute-start(bf16[8,4,2,1024]{3,2,1,0:T(2,128)(2,1)S(1)} %get-tuple-element.138), channel_id=1, source_target_pairs={{8,0},{16,8},{24,16},{32,24},{40,32},{48,40},{56,48},{64,56},{72,6... | collective-permute-start | bytes 393224 | tf_op jit(solution)/shard_map/ppermute | solution.py:22
  560.0 5.9 %collective-permute-start.10 = (bf16[8,4,20,2]{3,2,1,0:T(8,128)(2,1)S(1)}, bf16[8,4,20,2]{3,2,1,0:T(8,128)(2,1)S(1)}, u32[]{:S(2)}, u32[]{:S(2)}) collective-permute-start(bf16[8,4,20,2]{3,2,1,0:T(8,128)(2,1)S(1)} %get-tuple-element.127), channel_id=1, source_target_pairs={{0,1},{1,2},{2,3},{3,4},{4,5},{5,6},{6,7},{8,9},{9,10},{10,11},{11... | collective-permute-start | bytes 7688 | tf_op jit(solution)/shard_map/ppermute | solution.py:21
  563.3 7.0 %collective-permute-start.11 = (bf16[8,4,20,2]{3,2,1,0:T(8,128)(2,1)S(1)}, bf16[8,4,20,2]{3,2,1,0:T(8,128)(2,1)S(1)}, u32[]{:S(2)}, u32[]{:S(2)}) collective-permute-start(bf16[8,4,20,2]{3,2,1,0:T(8,128)(2,1)S(1)} %get-tuple-element.128), channel_id=1, source_target_pairs={{1,0},{2,1},{3,2},{4,3},{5,4},{6,5},{7,6},{9,8},{10,9},{11,10},{12... | collective-permute-start | bytes 7688 | tf_op jit(solution)/shard_map/ppermute | solution.py:22
where the time goes:
time: 588 us; the launch traced here: 586 us
  blocking collectives  444 us (76%)
  other arithmetic  61.4 us (10%)
  starting transfers between devices  34.6 us (6%)
  waiting for transfers between devices  31.4 us (5%)
  matrix products  6.88 us (1%)
    psum x5, blocking collectives, per_device(): sums = lax.psum(moments(share, centers, mean, var, weight), ('gy', 'gx'))  369 us
    unnamed x1, blocking collectives  75.7 us
    reduce_max x3, other arithmetic, per_device(): q = jax.nn.softmax(unary + BETA * field, axis=0).astype(jnp.bfloat16)  33.8 us
    ppermute x6, waiting for transfers between devices, extended(): after = lax.ppermute(initial, axis, down)  30.3 us
    ppermute x6, starting transfers between devices, extended(): before = lax.ppermute(last, axis, up)  19.8 us
    ppermute x6, starting transfers between devices, extended(): after = lax.ppermute(initial, axis, down)  14.8 us
  transfers between devices with their start and end apart: 12, of which 11 were waited for; matrix products, arithmetic and copies ran while one was open for 0% of the time, Pallas kernels for 0%

commit v1 on v0

--- a/solution.py
+++ b/solution.py
@@ -106,7 +106,9 @@
     density = share * scale_factor
     centers = ((start + jnp.arange(share.shape[0], dtype=jnp.int32)).astype(jnp.float32) + 0.5) / NB
     for step in range(EM_ITERS):
-        sums = lax.psum(moments(share, centers, mean, var, weight), ("gy", "gx"))
+        sums = jnp.sum(
+            lax.all_gather(moments(share, centers, mean, var, weight), ("gy", "gx")), axis=0
+        )
         mean, var, weight = refit(sums, float(phases))
     params = jnp.stack([mean, var, weight])
     intensity = (bins.astype(jnp.float32) + 0.5) / NB

time: 588 us -> 552 us (0.939)
  blocking collectives: 444 us -> 406 us
    psum x5 -> x0, blocking collectives: 369 us -> none  [per_device(): sums = lax.psum(moments(share, centers, mean, var, weight), ('gy', 'gx'))]
    all_gather x0 -> x5, blocking collectives: none -> 330 us  [per_device(): lax.all_gather(moments(share, centers, mean, var, weight), ('gy', 'gx'))]
where the time goes in v1:
time: 552 us; the launch traced here: 551 us
  blocking collectives  406 us (74%)
  other arithmetic  64.7 us (12%)
  starting transfers between devices  34.1 us (6%)
  waiting for transfers between devices  32.4 us (6%)
  matrix products  6.88 us (1%)
    all_gather x5, blocking collectives, per_device(): lax.all_gather(moments(share, centers, mean, var, weight), ('gy', 'gx'))  330 us
    unnamed x1, blocking collectives  75.7 us
    reduce_max x3, other arithmetic, per_device(): q = jax.nn.softmax(unary + BETA * field, axis=0).astype(jnp.bfloat16)  33.8 us
    ppermute x6, waiting for transfers between devices, extended(): after = lax.ppermute(initial, axis, down)  30.6 us
    ppermute x6, starting transfers between devices, extended(): before = lax.ppermute(last, axis, up)  19.4 us
    ppermute x6, starting transfers between devices, extended(): after = lax.ppermute(initial, axis, down)  14.6 us
  transfers between devices with their start and end apart: 12, of which 11 were waited for; matrix products, arithmetic and copies ran while one was open for 0% of the time, Pallas kernels for 0%

profile of v1, /device:TPU:121, one launch (start us, length us, event | category | flops | bytes accessed | tf_op | source)
XLA Modules:
  0.0 551.1 jit_solution(5134748434429618262)
XLA Ops:
  7.1 10.4 %while.13 = (s32[]{:T(128)}, f32[32,128]{1,0:T(8,128)S(1)}, s32[4,16384]{1,0:T(4,128)S(1)}, s32[4,16384]{1,0:T(4,128)S(1)}, s32[]{:T(128)}, /*index=5*/s32[]{:T(128)}) while((s32[]{:T(128)}, f32[32,128]{1,0:T(8,128)S(1)}, s32[4,16384]{1,0:T(4,128)S(1)}, s32[4,16384]{1,0:T(4,128)S(1)}, s32[]{:T(128)}, /*index=5*/s32[]{:T(128)}) %tuple.78), condition=%wide.region_3.4_spmd.clone, body=%wide.region_2.3_spmd.clone.sunk | while | flops 137715712 | bytes 2719839 | solution.py:97
  17.4 75.7 %all-reduce.3 = f32[4096]{0:T(1024)S(1)} all-reduce(f32[4096]{0:T(1024)S(1)} %bitcast.185), channel_id=7, replica_groups=mesh['gy'=32,'gx'=8] {'gy','gx'}, use_global_device_ids=true, to_apply=%region_4.5.clone | all-reduce | flops 4096 | bytes 32768
  94.0 66.7 %all-gather.5 = f32[256,3,8]{2,1,0:T(4,128)S(1)} all-gather(f32[1,3,8]{2,1,0:T(4,128)S(1)} %maximum_bitcast_fusion), channel_id=2, replica_groups=mesh['gy'=32,'gx'=8] {'gy','gx'}, dimensions={0}, use_global_device_ids=true | all-gather | bytes 24672 | tf_op jit(solution)/shard_map/all_gather | solution.py:110
  162.7 65.8 %all-gather.6 = f32[256,3,8]{2,1,0:T(4,128)S(1)} all-gather(f32[1,3,8]{2,1,0:T(4,128)S(1)} %maximum_bitcast_fusion.1), channel_id=3, replica_groups=mesh['gy'=32,'gx'=8] {'gy','gx'}, dimensions={0}, use_global_device_ids=true | all-gather | bytes 24672 | tf_op jit(solution)/shard_map/all_gather | solution.py:110
  230.6 65.7 %all-gather.7 = f32[256,3,8]{2,1,0:T(4,128)S(1)} all-gather(f32[1,3,8]{2,1,0:T(4,128)S(1)} %maximum_bitcast_fusion.2), channel_id=4, replica_groups=mesh['gy'=32,'gx'=8] {'gy','gx'}, dimensions={0}, use_global_device_ids=true | all-gather | bytes 24672 | tf_op jit(solution)/shard_map/all_gather | solution.py:110
  298.3 65.7 %all-gather.8 = f32[256,3,8]{2,1,0:T(4,128)S(1)} all-gather(f32[1,3,8]{2,1,0:T(4,128)S(1)} %maximum_bitcast_fusion.3), channel_id=5, replica_groups=mesh['gy'=32,'gx'=8] {'gy','gx'}, dimensions={0}, use_global_device_ids=true | all-gather | bytes 24672 | tf_op jit(solution)/shard_map/all_gather | solution.py:110
  366.0 65.9 %all-gather.9 = f32[256,3,8]{2,1,0:T(4,128)S(1)} all-gather(f32[1,3,8]{2,1,0:T(4,128)S(1)} %maximum_bitcast_fusion.4), channel_id=6, replica_groups=mesh['gy'=32,'gx'=8] {'gy','gx'}, dimensions={0}, use_global_device_ids=true | all-gather | bytes 24672 | tf_op jit(solution)/shard_map/all_gather | solution.py:110
  435.9 4.3 collective-permute-start
  442.9 7.2 %collective-permute-done.1 = bf16[8,4,2,1024]{3,2,1,0:T(2,128)(2,1)S(1)} collective-permute-done((bf16[8,4,2,1024]{3,2,1,0:T(2,128)(2,1)S(1)}, bf16[8,4,2,1024]{3,2,1,0:T(2,128)(2,1)S(1)}, u32[]{:S(2)}, u32[]{:S(2)}) %collective-permute-start.1) | collective-permute-done | bytes 131104 | tf_op jit(solution)/shard_map/ppermute | solution.py:22
  450.3 3.6 collective-permute-start.2
  456.5 4.4 collective-permute-done.3
  460.9 2.9 maximum_maximum_fusion
  463.8 11.3 %fusion.75 = (f32[4,16,1024]{2,1,0:T(8,128)S(1)}, f32[8,4,16,1024]{3,2,1,0:T(8,128)S(1)}) fusion(f32[8,6,16,1024]{3,2,1,0:T(8,128)S(1)} %pad_convert_fusion.2, bf16[8,4,20,1026]{3,2,1,0:T(8,128)(2,1)S(1)} %get-tuple-element.134, bf16[8,4,2,1024]{3,2,1,0:T(2,128)(2,1)S(1)} %collective-permute-done.1, bf16[8,4,16,1024]{3,2,1,0:T(8,128)(2,1)S(1)} %multiply_convert_fusion.3, ...), kind=kLoop, calls=%fused_computation.201 | loop fusion | flops 47120384 | bytes 30146656 | tf_op jit(solution)/shard_map/reduce_max | solution.py:122
  478.0 3.4 collective-permute-start.5
  481.8 5.2 collective-permute-done.5
  487.3 4.2 collective-permute-start.6
  494.0 4.4 collective-permute-done.7
  501.3 11.3 %fusion.73 = (f32[4,16,1024]{2,1,0:T(8,128)S(1)}, f32[8,4,16,1024]{3,2,1,0:T(8,128)S(1)}) fusion(f32[8,6,16,1024]{3,2,1,0:T(8,128)S(1)} %pad_convert_fusion.1, bf16[8,4,20,1026]{3,2,1,0:T(8,128)(2,1)S(1)} %get-tuple-element.130, bf16[8,4,2,1024]{3,2,1,0:T(2,128)(2,1)S(1)} %collective-permute-done.5, bf16[8,4,16,1024]{3,2,1,0:T(8,128)(2,1)S(1)} %multiply_convert_fusion.2, ...), kind=kLoop, calls=%fused_computation.200 | loop fusion | flops 47120384 | bytes 30146656 | tf_op jit(solution)/shard_map/reduce_max | solution.py:122
  515.5 3.4 collective-permute-start.9
  519.5 5.1 collective-permute-done.9
  524.8 3.5 collective-permute-start.10
  530.9 4.4 collective-permute-done.11
  535.3 2.9 maximum_maximum_fusion.2
  538.2 11.3 %fusion.71 = (f32[4,16,1024]{2,1,0:T(8,128)S(1)}, f32[8,4,16,1024]{3,2,1,0:T(8,128)S(1)}) fusion(f32[8,6,16,1024]{3,2,1,0:T(8,128)S(1)} %pad_convert_fusion, bf16[8,4,20,1026]{3,2,1,0:T(8,128)(2,1)S(1)} %get-tuple-element.126, bf16[8,4,2,1024]{3,2,1,0:T(2,128)(2,1)S(1)} %collective-permute-done.9, bf16[8,4,16,1024]{3,2,1,0:T(8,128)(2,1)S(1)} %multiply_convert_fusion.1, ...), kind=kLoop, calls=%fused_computation.199 | loop fusion | flops 47120384 | bytes 30146656 | tf_op jit(solution)/shard_map/reduce_max | solution.py:122
  (105 shorter events, 48.5 us)
Async XLA Ops:
  7.0 86.7 %copy-start.1 = (f32[8]{0:T(128)S(1)}, f32[8]{0:T(128)}, u32[]{:S(2)}) copy-start(f32[8]{0:T(128)} %param.10) | copy-start | bytes 100
  162.7 270.8 %copy-start = (bf16[8,4,16,1024]{3,2,1,0:T(8,128)(2,1)S(1)}, bf16[8,4,16,1024]{3,2,1,0:T(8,128)(2,1)}, u32[]{:S(2)}) copy-start(bf16[8,4,16,1024]{3,2,1,0:T(8,128)(2,1)} %param.9) | copy-start | bytes 3145732
  435.9 6.9 %collective-permute-start = (bf16[8,4,2,1024]{3,2,1,0:T(2,128)(2,1)S(1)}, bf16[8,4,2,1024]{3,2,1,0:T(2,128)(2,1)S(1)}, u32[]{:S(2)}, u32[]{:S(2)}) collective-permute-start(bf16[8,4,2,1024]{3,2,1,0:T(2,128)(2,1)S(1)} %get-tuple-element.141), channel_id=1, source_target_pairs={{0,8},{8,16},{16,24},{24,32},{32,40},{40,48},{48,56},{56,64},{64,7... | collective-permute-start | bytes 393224 | tf_op jit(solution)/shard_map/ppermute | solution.py:21
  440.2 9.8 %collective-permute-start.1 = (bf16[8,4,2,1024]{3,2,1,0:T(2,128)(2,1)S(1)}, bf16[8,4,2,1024]{3,2,1,0:T(2,128)(2,1)S(1)}, u32[]{:S(2)}, u32[]{:S(2)}) collective-permute-start(bf16[8,4,2,1024]{3,2,1,0:T(2,128)(2,1)S(1)} %get-tuple-element.142), channel_id=1, source_target_pairs={{8,0},{16,8},{24,16},{32,24},{40,32},{48,40},{56,48},{64,56},{72,6... | collective-permute-start | bytes 393224 | tf_op jit(solution)/shard_map/ppermute | solution.py:22
  450.3 6.2 %collective-permute-start.2 = (bf16[8,4,20,2]{3,2,1,0:T(8,128)(2,1)S(1)}, bf16[8,4,20,2]{3,2,1,0:T(8,128)(2,1)S(1)}, u32[]{:S(2)}, u32[]{:S(2)}) collective-permute-start(bf16[8,4,20,2]{3,2,1,0:T(8,128)(2,1)S(1)} %get-tuple-element.135), channel_id=1, source_target_pairs={{0,1},{1,2},{2,3},{3,4},{4,5},{5,6},{6,7},{8,9},{9,10},{10,11},{11... | collective-permute-start | bytes 7688 | tf_op jit(solution)/shard_map/ppermute | solution.py:21
  453.9 7.0 %collective-permute-start.3 = (bf16[8,4,20,2]{3,2,1,0:T(8,128)(2,1)S(1)}, bf16[8,4,20,2]{3,2,1,0:T(8,128)(2,1)S(1)}, u32[]{:S(2)}, u32[]{:S(2)}) collective-permute-start(bf16[8,4,20,2]{3,2,1,0:T(8,128)(2,1)S(1)} %get-tuple-element.136), channel_id=1, source_target_pairs={{1,0},{2,1},{3,2},{4,3},{5,4},{6,5},{7,6},{9,8},{10,9},{11,10},{12... | collective-permute-start | bytes 7688 | tf_op jit(solution)/shard_map/ppermute | solution.py:22
  476.1 5.7 %collective-permute-start.4 = (bf16[8,4,2,1024]{3,2,1,0:T(2,128)(2,1)S(1)}, bf16[8,4,2,1024]{3,2,1,0:T(2,128)(2,1)S(1)}, u32[]{:S(2)}, u32[]{:S(2)}) collective-permute-start(bf16[8,4,2,1024]{3,2,1,0:T(2,128)(2,1)S(1)} %get-tuple-element.139), channel_id=1, source_target_pairs={{0,8},{8,16},{16,24},{24,32},{32,40},{40,48},{48,56},{56,64},{64,7... | collective-permute-start | bytes 393224 | tf_op jit(solution)/shard_map/ppermute | solution.py:21
  478.0 9.0 %collective-permute-start.5 = (bf16[8,4,2,1024]{3,2,1,0:T(2,128)(2,1)S(1)}, bf16[8,4,2,1024]{3,2,1,0:T(2,128)(2,1)S(1)}, u32[]{:S(2)}, u32[]{:S(2)}) collective-permute-start(bf16[8,4,2,1024]{3,2,1,0:T(2,128)(2,1)S(1)} %get-tuple-element.140), channel_id=1, source_target_pairs={{8,0},{16,8},{24,16},{32,24},{40,32},{48,40},{56,48},{64,56},{72,6... | collective-permute-start | bytes 393224 | tf_op jit(solution)/shard_map/ppermute | solution.py:22
  487.3 6.8 %collective-permute-start.6 = (bf16[8,4,20,2]{3,2,1,0:T(8,128)(2,1)S(1)}, bf16[8,4,20,2]{3,2,1,0:T(8,128)(2,1)S(1)}, u32[]{:S(2)}, u32[]{:S(2)}) collective-permute-start(bf16[8,4,20,2]{3,2,1,0:T(8,128)(2,1)S(1)} %get-tuple-element.131), channel_id=1, source_target_pairs={{0,1},{1,2},{2,3},{3,4},{4,5},{5,6},{6,7},{8,9},{9,10},{10,11},{11... | collective-permute-start | bytes 7688 | tf_op jit(solution)/shard_map/ppermute | solution.py:21
  491.4 7.0 %collective-permute-start.7 = (bf16[8,4,20,2]{3,2,1,0:T(8,128)(2,1)S(1)}, bf16[8,4,20,2]{3,2,1,0:T(8,128)(2,1)S(1)}, u32[]{:S(2)}, u32[]{:S(2)}) collective-permute-start(bf16[8,4,20,2]{3,2,1,0:T(8,128)(2,1)S(1)} %get-tuple-element.132), channel_id=1, source_target_pairs={{1,0},{2,1},{3,2},{4,3},{5,4},{6,5},{7,6},{9,8},{10,9},{11,10},{12... | collective-permute-start | bytes 7688 | tf_op jit(solution)/shard_map/ppermute | solution.py:22
  513.6 5.9 %collective-permute-start.8 = (bf16[8,4,2,1024]{3,2,1,0:T(2,128)(2,1)S(1)}, bf16[8,4,2,1024]{3,2,1,0:T(2,128)(2,1)S(1)}, u32[]{:S(2)}, u32[]{:S(2)}) collective-permute-start(bf16[8,4,2,1024]{3,2,1,0:T(2,128)(2,1)S(1)} %get-tuple-element.137), channel_id=1, source_target_pairs={{0,8},{8,16},{16,24},{24,32},{32,40},{40,48},{48,56},{56,64},{64,7... | collective-permute-start | bytes 393224 | tf_op jit(solution)/shard_map/ppermute | solution.py:21
  515.5 9.0 %collective-permute-start.9 = (bf16[8,4,2,1024]{3,2,1,0:T(2,128)(2,1)S(1)}, bf16[8,4,2,1024]{3,2,1,0:T(2,128)(2,1)S(1)}, u32[]{:S(2)}, u32[]{:S(2)}) collective-permute-start(bf16[8,4,2,1024]{3,2,1,0:T(2,128)(2,1)S(1)} %get-tuple-element.138), channel_id=1, source_target_pairs={{8,0},{16,8},{24,16},{32,24},{40,32},{48,40},{56,48},{64,56},{72,6... | collective-permute-start | bytes 393224 | tf_op jit(solution)/shard_map/ppermute | solution.py:22
  524.8 6.1 %collective-permute-start.10 = (bf16[8,4,20,2]{3,2,1,0:T(8,128)(2,1)S(1)}, bf16[8,4,20,2]{3,2,1,0:T(8,128)(2,1)S(1)}, u32[]{:S(2)}, u32[]{:S(2)}) collective-permute-start(bf16[8,4,20,2]{3,2,1,0:T(8,128)(2,1)S(1)} %get-tuple-element.127), channel_id=1, source_target_pairs={{0,1},{1,2},{2,3},{3,4},{4,5},{5,6},{6,7},{8,9},{9,10},{10,11},{11... | collective-permute-start | bytes 7688 | tf_op jit(solution)/shard_map/ppermute | solution.py:21
  528.3 7.0 %collective-permute-start.11 = (bf16[8,4,20,2]{3,2,1,0:T(8,128)(2,1)S(1)}, bf16[8,4,20,2]{3,2,1,0:T(8,128)(2,1)S(1)}, u32[]{:S(2)}, u32[]{:S(2)}) collective-permute-start(bf16[8,4,20,2]{3,2,1,0:T(8,128)(2,1)S(1)} %get-tuple-element.128), channel_id=1, source_target_pairs={{1,0},{2,1},{3,2},{4,3},{5,4},{6,5},{7,6},{9,8},{10,9},{11,10},{12... | collective-permute-start | bytes 7688 | tf_op jit(solution)/shard_map/ppermute | solution.py:22
